TPU v7x, 32 devices: a whole 2x2x4 slice. The times are simulated.
32 devices in a mesh: row: 4 (over y, core), col: 8 (over z, x).
Axes of the slice: x: 2, y: 2, z: 4, core: 2. Of those that a mesh axis runs over, the one named last changes fastest.
Arguments:
- outside: bfloat16 [2048, 4096], P('row', 'col'), may hold values from 0.0099 to 17.5
- inside_head: bfloat16 [2048, 4096], P('row', 'col'), may hold values from 0.0099 to 17.5
- inside_tail: bfloat16 [2048, 4096], P('row', 'col'), may hold values from 0.0099 to 17.5
- inside_pair: float32 [512, 4096], P(None, 'col'), may hold values from 0.4 to 1.6
- seq_head: int32 [1, 4096], P(None, 'col'), may hold values from 0 to 3
- seq_tail: int32 [1, 4096], P(None, 'col'), may hold values from 0 to 3
- pair_mask: int32 [4, 32], P(None, 'col'), may hold values 0 or 1
- split_weight: float32 [4], replicated, may hold values from 0.5 to 2
- pair_weight: float32 [4, 4], replicated, may hold values from 0.5 to 2
- span_blocks: int32 [1], replicated, may hold values from 8 to 63
- partition: float32 [1], replicated, may hold values from 1 to 3
Outputs:
- outside_out: float32 [2048, 4096], P('row', 'col')
- prob_out: float32 [2048, 4096], P('row', 'col')
All inputs are finite; a program needn't handle non-finite values. No bound on the sum of `pair_mask` on one device may be relied on, other than what follows from the above.
Results may differ from a plain program's by a relative error of at most 0.0003.
Values may be sent and summed in bfloat16 or wider, within the bound.
No kernel may reach another device: no remote copies, remote signals or barrier semaphores. Data moves between devices by JAX's collectives and lax.ppermute only.
A program may use at most 64 MiB of HBM per device.

v0:
```python
import jax
import jax.numpy as jnp
from jax import lax
from jax.sharding import PartitionSpec as P

precise = lax.Precision.HIGHEST


def passed_along(x, axis, by):
    length = lax.axis_size(axis)
    return lax.ppermute(x, axis, [(i, (i + by) % length) for i in range(length)])


def finish(
    right_sum,
    left_sum,
    head_codes,
    tail_codes,
    mask_rows,
    pair_rows,
    split_weight,
    pair_weight,
    span_blocks,
    partition,
    owner_factor,
):
    cycles, tile_size = head_codes.shape
    repeat = tile_size // mask_rows.shape[1]
    allowed = jnp.repeat(
        jnp.repeat(mask_rows.astype(jnp.float32), repeat, axis=0), repeat, axis=1
    ).reshape(cycles, tile_size, tile_size)
    letters = jnp.arange(4, dtype=jnp.int32)
    head_hot = (head_codes[:, :, None] == letters[None, None, :]).astype(jnp.float32)
    tail_hot = (tail_codes[:, :, None] == letters[None, None, :]).astype(jnp.float32)
    head_weight = jnp.einsum("mak,k->ma", head_hot, split_weight, precision=precise)
    tail_weight = jnp.einsum("mak,k->ma", tail_hot, split_weight, precision=precise)
    outside_diag = (
        owner_factor
        * allowed
        * (right_sum * tail_weight[:, None, :] + head_weight[:, :, None] * left_sum)
        / tile_size
    )
    pair_table = jnp.einsum("mak,kl,mbl->mab", head_hot, pair_weight, tail_hot, precision=precise)
    positions = jnp.arange(tile_size, dtype=jnp.float32)
    span_nt = (
        tile_size * span_blocks[0].astype(jnp.float32) + positions[None, :] - positions[:, None]
    )
    penalty = jnp.sqrt(64.0 * tile_size / span_nt)
    pair_prob = (
        pair_rows.reshape(cycles, tile_size, tile_size)
        * outside_diag
        * pair_table
        * penalty[None, :, :]
        / partition[0]
    )
    return (
        outside_diag.reshape(cycles * tile_size, tile_size),
        pair_prob.reshape(cycles * tile_size, tile_size),
    )


def as_tiles(array):
    return array.reshape(-1, array.shape[1], array.shape[1])


def move_later(stack):
    return jnp.concatenate([jnp.zeros_like(stack), stack[:-1]], axis=0)


def per_device(
    outside,
    inside_head,
    inside_tail,
    inside_pair,
    seq_head,
    seq_tail,
    pair_mask,
    split_weight,
    pair_weight,
    span_blocks,
    partition,
):
    row_count = lax.axis_size("row")
    row_id = lax.axis_index("row")
    col_id = lax.axis_index("col")
    out_tiles = as_tiles(outside)
    right_part = jnp.einsum(
        "mac,mbc->mab", out_tiles, as_tiles(inside_tail), preferred_element_type=jnp.float32
    )
    window = passed_along(right_part, "col", -1)
    for level in range(row_count.bit_length() - 1):
        window = window + passed_along(window, "col", -(1 << level))
    reach = (col_id - row_id) % row_count
    reach = jnp.where(reach == 0, row_count, reach)
    left_part = jnp.einsum(
        "mca,mcb->mab", as_tiles(inside_head), out_tiles, preferred_element_type=jnp.float32
    )
    left_part = jnp.where(col_id < reach, move_later(left_part), left_part)
    left_sum = lax.psum(left_part, "row")
    owner_factor = (row_id == col_id % row_count).astype(jnp.float32)
    return finish(
        window,
        left_sum,
        seq_head,
        seq_tail,
        pair_mask,
        inside_pair,
        split_weight,
        pair_weight,
        span_blocks,
        partition,
        owner_factor,
    )


def solution(mesh):
    placed = (
        P("row", "col"),
        P("row", "col"),
        P("row", "col"),
        P(None, "col"),
        P(None, "col"),
        P(None, "col"),
        P(None, "col"),
        P(),
        P(),
        P(),
        P(),
    )
    return jax.shard_map(
        per_device,
        mesh=mesh,
        in_specs=placed,
        out_specs=(P("row", "col"), P("row", "col")),
        check_vma=False,
    )
```

profile of v0, /device:TPU:0, one launch (start us, length us, event | category | flops | bytes accessed | tf_op | source)
XLA Modules:
  0.0 118.1 jit_solution(13893284041892178920)
XLA Ops:
  7.2 0.0 copy-start
  7.2 0.0 all-reduce.2.cloned.1.call-start
  7.2 1.0 copy-done
  8.2 1.5 %convolution_bitcast_fusion.1 = f32[1,512,512]{2,1,0:T(8,128)S(1)} fusion(bf16[512,512]{1,0:T(8,128)(2,1)S(1)} %copy-done, bf16[512,512]{1,0:T(8,128)(2,1)} %param.13), kind=kOutput, calls=%fused_computation.3 | convolution fusion | flops 268435456 | bytes 2097152 | tf_op jit(solution)/shard_map/mac,mbc->mab/dot_general | solution.py:87
  9.7 6.1 %collective-permute-start = (f32[1,512,512]{2,1,0:T(8,128)S(1)}, f32[1,512,512]{2,1,0:T(8,128)S(1)}, u32[]{:S(2)}, u32[]{:S(2)}) collective-permute-start(f32[1,512,512]{2,1,0:T(8,128)S(1)} %convolution_bitcast_fusion.1), channel_id=1, source_target_pairs={{0,7},{1,0},{2,1},{3,2},{4,3},{5,4},{6,5},{7,6},{8,15},{9,8},{10,9... | collective-permute-start | bytes 3145736 | tf_op jit(solution)/shard_map/ppermute | solution.py:11
  15.8 22.4 %collective-permute-done = f32[1,512,512]{2,1,0:T(8,128)S(1)} collective-permute-done((f32[1,512,512]{2,1,0:T(8,128)S(1)}, f32[1,512,512]{2,1,0:T(8,128)S(1)}, u32[]{:S(2)}, u32[]{:S(2)}) %collective-permute-start) | collective-permute-done | bytes 1048608 | tf_op jit(solution)/shard_map/ppermute | solution.py:11
  38.2 5.2 %collective-permute-start.1 = (f32[1,512,512]{2,1,0:T(8,128)S(1)}, f32[1,512,512]{2,1,0:T(8,128)}, u32[]{:S(2)}, u32[]{:S(2)}) collective-permute-start(f32[1,512,512]{2,1,0:T(8,128)S(1)} %collective-permute-done), channel_id=1, source_target_pairs={{0,7},{1,0},{2,1},{3,2},{4,3},{5,4},{6,5},{7,6},{8,15},{9,8},{10,9... | collective-permute-start | bytes 3145736 | tf_op jit(solution)/shard_map/ppermute | solution.py:11
  43.4 0.0 copy-start.6
  43.4 21.6 %collective-permute-done.1 = f32[1,512,512]{2,1,0:T(8,128)} collective-permute-done((f32[1,512,512]{2,1,0:T(8,128)S(1)}, f32[1,512,512]{2,1,0:T(8,128)}, u32[]{:S(2)}, u32[]{:S(2)}) %collective-permute-start.1) | collective-permute-done | bytes 1048608 | tf_op jit(solution)/shard_map/ppermute | solution.py:11
  64.9 1.4 %add.30 = f32[1,512,512]{2,1,0:T(8,128)S(1)} add(f32[1,512,512]{2,1,0:T(8,128)S(1)} %collective-permute-done, f32[1,512,512]{2,1,0:T(8,128)} %collective-permute-done.1) | non-fusion elementwise | flops 262144 | bytes 3145728 | tf_op jit(solution)/shard_map/add | solution.py:92
  66.4 1.5 %collective-permute-start.2 = (f32[1,512,512]{2,1,0:T(8,128)S(1)}, f32[1,512,512]{2,1,0:T(8,128)}, u32[]{:S(2)}, u32[]{:S(2)}) collective-permute-start(f32[1,512,512]{2,1,0:T(8,128)S(1)} %add.30), channel_id=1, source_target_pairs={{0,6},{1,7},{2,0},{3,1},{4,2},{5,3},{6,4},{7,5},{8,14},{9,15},{10,... | collective-permute-start | bytes 3145736 | tf_op jit(solution)/shard_map/ppermute | solution.py:11
  67.8 0.0 copy-done.6
  67.8 1.4 %fusion = f32[1,512,512]{2,1,0:T(8,128)} fusion(bf16[512,512]{1,0:T(8,128)(2,1)S(1)} %copy-done.6, bf16[512,512]{1,0:T(8,128)(2,1)S(1)} %copy-done, pred[]{:T(512)S(6)} %lt.15), kind=kOutput, calls=%fused_computation.1 | convolution fusion | flops 268697600 | bytes 2097153 | tf_op jit(solution)/shard_map/mca,mcb->mab/dot_general | solution.py:95
  69.3 0.0 all-reduce.2.cloned.1.call-update
  69.3 0.0 copy-start.4
  69.3 0.7 copy-done.4
  70.0 0.6 broadcast_in_dim.7
  70.6 1.4 %mul.59 = f32[1,512,512]{2,1,0:T(8,128)} reshape(f32[512,4,128]{2,1,0:T(4,128)S(1)} %broadcast_in_dim.7) | data formatting | bytes 2097152 | tf_op jit(solution)/shard_map/mul | solution.py:38
  73.3 0.0 copy-start.7
  73.3 0.0 copy-start.8
  73.3 0.7 copy-done.7
  74.0 0.0 copy-done.8
  74.0 0.3 fusion.7
  74.3 0.0 copy-start.2
  74.3 0.7 copy-done.2
  75.0 0.0 copy-start.3
  75.0 0.3 fusion.6
  75.3 0.4 copy-done.3
  75.7 0.3 fusion.5
  76.0 30.8 %all-reduce.2.cloned.1.call-done = f32[1,512,512]{2,1,0:T(8,128)} async-done(((f32[1,512,512]{2,1,0:T(8,128)}), f32[1,512,512]{2,1,0:T(8,128)}) %all-reduce.2.cloned.1.call-update) | async-done | bytes 1048592 | tf_op jit(solution)/shard_map/psum | solution.py:99
  106.9 0.0 collective-permute-done.2
  106.9 0.0 copy-start.5
  106.9 2.2 %multiply_multiply_fusion = f32[1,512,512]{2,1,0:T(8,128)S(1)} fusion(f32[1,512,512]{2,1,0:T(8,128)} %mul.59, f32[1,512,512]{2,1,0:T(8,128)} %all-reduce.2.cloned.1.call-done, f32[1,512,512]{2,1,0:T(8,128)S(1)} %add.30, f32[1,512,512]{2,1,0:T(8,128)} %collective-permute-done.2, f32[512]{0:T(512)S(1)} %bitcast.46, f32[512]{0:T(512)S(1)} %bitcast.45), kind=kLoop, calls=%fused_computation.9 | loop fusion | flops 1572864 | bytes 5246976 | tf_op jit(solution)/shard_map/div | solution.py:38
  109.1 0.0 copy-start.1
  109.1 0.0 copy-done.5
  109.1 2.2 %fusion.4 = f32[512,512]{1,0:T(8,128)} fusion(f32[512,4]{1,0:T(8,128)S(1)} %fusion.5, f32[1,512,512]{2,1,0:T(8,128)S(1)} %multiply_multiply_fusion, f32[512,512]{1,0:T(8,128)S(1)} %copy-done.5, f32[]{:T(128)} %bitcast.40, f32[512]{0:T(512)S(1)} %iota_add_fusion, s32[512]{0:T(512)S(1)} %bitcast.48), kind=kOutput, calls=%fused_computation.7 | convolution fusion | flops 14157824 | bytes 3158020 | tf_op jit(solution)/shard_map/mak,kl,mbl->mab/dot_general | solution.py:43
  111.3 0.0 copy-done.1
  (3 shorter events, 0.0 us)
Async XLA Ops:
  7.2 1.0 copy-start
  7.2 99.7 %all-reduce.2.cloned.1.call-start = ((), (), s32[]{:S(2)}) async-start(), calls=%async_computation | async-start | bytes 2097152 | tf_op jit(solution)/shard_map/psum | solution.py:99
  9.7 28.5 %collective-permute-start = (f32[1,512,512]{2,1,0:T(8,128)S(1)}, f32[1,512,512]{2,1,0:T(8,128)S(1)}, u32[]{:S(2)}, u32[]{:S(2)}) collective-permute-start(f32[1,512,512]{2,1,0:T(8,128)S(1)} %convolution_bitcast_fusion.1), channel_id=1, source_target_pairs={{0,7},{1,0},{2,1},{3,2},{4,3},{5,4},{6,5},{7,6},{8,15},{9,8},{10,9... | collective-permute-start | bytes 3145736 | tf_op jit(solution)/shard_map/ppermute | solution.py:11
  38.2 26.7 %collective-permute-start.1 = (f32[1,512,512]{2,1,0:T(8,128)S(1)}, f32[1,512,512]{2,1,0:T(8,128)}, u32[]{:S(2)}, u32[]{:S(2)}) collective-permute-start(f32[1,512,512]{2,1,0:T(8,128)S(1)} %collective-permute-done), channel_id=1, source_target_pairs={{0,7},{1,0},{2,1},{3,2},{4,3},{5,4},{6,5},{7,6},{8,15},{9,8},{10,9... | collective-permute-start | bytes 3145736 | tf_op jit(solution)/shard_map/ppermute | solution.py:11
  43.4 24.5 %copy-start.6 = (bf16[512,512]{1,0:T(8,128)(2,1)S(1)}, bf16[512,512]{1,0:T(8,128)(2,1)}, u32[]{:S(2)}) copy-start(bf16[512,512]{1,0:T(8,128)(2,1)} %param.12) | copy-start | bytes 1572868
  66.4 40.5 %collective-permute-start.2 = (f32[1,512,512]{2,1,0:T(8,128)S(1)}, f32[1,512,512]{2,1,0:T(8,128)}, u32[]{:S(2)}, u32[]{:S(2)}) collective-permute-start(f32[1,512,512]{2,1,0:T(8,128)S(1)} %add.30), channel_id=1, source_target_pairs={{0,6},{1,7},{2,0},{3,1},{4,2},{5,3},{6,4},{7,5},{8,14},{9,15},{10,... | collective-permute-start | bytes 3145736 | tf_op jit(solution)/shard_map/ppermute | solution.py:11
  69.3 0.7 copy-start.4
  73.3 0.7 copy-start.7
  73.3 0.7 copy-start.8
  74.3 0.7 copy-start.2
  75.0 0.7 copy-start.3
  106.9 2.2 %copy-start.5 = (f32[512,512]{1,0:T(8,128)S(1)}, f32[512,512]{1,0:T(8,128)}, u32[]{:S(2)}) copy-start(f32[512,512]{1,0:T(8,128)} %param.14) | copy-start | bytes 3145732
  109.1 2.2 %copy-start.1 = (f32[1,512,512]{2,1,0:T(8,128)}, f32[1,512,512]{2,1,0:T(8,128)S(1)}, u32[]{:S(2)}) copy-start(f32[1,512,512]{2,1,0:T(8,128)S(1)} %multiply_multiply_fusion) | copy-start | bytes 3145732
Sparse Core Ops, SparseCore 0:
  69.4 37.4 all-reduce.1
where the time goes:
time: 118 us
  waiting for transfers between devices  74.8 us (63%)
  between operations  15.4 us (13%)
  starting transfers between devices  12.7 us (11%)
  matrix products  6.02 us (5%)
  local copies, waits for them, and re-layouts  5.42 us (5%)
  other arithmetic  3.66 us (3%)
    ppermute x3, waiting for transfers between devices, passed_along(): lax.ppermute(x, axis, [(i, (i + by) % length) for i in range(length)])  44 us
    psum x1, waiting for transfers between devices, per_device(): left_sum = lax.psum(left_part, 'row')  30.8 us
    ppermute x3, starting transfers between devices, passed_along(): lax.ppermute(x, axis, [(i, (i + by) % length) for i in range(length)])  12.7 us
    unnamed x18, local copies, waits for them, and re-layouts  3.4 us
    dot_general x2, matrix products, finish(): jnp.einsum('mak,kl,mbl->mab', head_hot, pair_weight, tail_hot, precision=...  2.47 us
  transfers between devices with their start and end apart: 4, of which 3 were waited for; matrix products, arithmetic and copies ran while one was open for 4% of the time, Pallas kernels for 0%

commit v1 on v0

--- a/solution.py
+++ b/solution.py
@@ -96,7 +96,7 @@
         "mca,mcb->mab", as_tiles(inside_head), out_tiles, preferred_element_type=jnp.float32
     )
     left_part = jnp.where(col_id < reach, move_later(left_part), left_part)
-    left_sum = lax.psum(left_part, "row")
+    left_sum = jnp.sum(lax.all_gather(left_part, "row"), axis=0)
     owner_factor = (row_id == col_id % row_count).astype(jnp.float32)
     return finish(
         window,

time: 118 us -> 103 us (0.87); the launches traced: 118 us -> 102 us
  waiting for transfers between devices: 74.8 us -> 57.8 us
  local copies, waits for them, and re-layouts: 5.42 us -> 3.03 us
  other arithmetic: 3.66 us -> 5.78 us
    psum x1 -> x0, waiting for transfers between devices: 30.8 us -> none  [per_device(): left_sum = lax.psum(left_part, 'row')]
    ppermute x3, waiting for transfers between devices: 44 us -> 57.7 us  [passed_along(): lax.ppermute(x, axis, [(i, (i + by) % length) for i in range(length)])]
    reduce_sum x0 -> x1, other arithmetic: none -> 3.76 us  [per_device(): left_sum = jnp.sum(lax.all_gather(left_part, 'row'), axis=0)]
    unnamed x18, local copies, waits for them, and re-layouts: 3.4 us -> 1.01 us
    add x1, other arithmetic: 1.43 us -> 0.21 us  [per_device(): window = window + passed_along(window, 'col', -(1 << level))]
  transfers between devices with their start and end apart: 4 -> 4, of which waited for: 3 -> 3; matrix products, arithmetic and copies ran while one was open for 4% -> 8% of each run, Pallas kernels for 0% -> 0%
where the time goes in v1:
time: 103 us; the launch traced here: 102 us
  waiting for transfers between devices  57.8 us (56%)
  between operations  15.6 us (15%)
  starting transfers between devices  12.6 us (12%)
  matrix products  7.14 us (7%)
  other arithmetic  5.78 us (6%)
  local copies, waits for them, and re-layouts  3.03 us (3%)
    ppermute x3, waiting for transfers between devices, passed_along(): lax.ppermute(x, axis, [(i, (i + by) % length) for i in range(length)])  57.7 us
    ppermute x3, starting transfers between devices, passed_along(): lax.ppermute(x, axis, [(i, (i + by) % length) for i in range(length)])  12.6 us
    reduce_sum x1, other arithmetic, per_device(): left_sum = jnp.sum(lax.all_gather(left_part, 'row'), axis=0)  3.76 us
    dot_general x2, matrix products, finish(): jnp.einsum('mak,kl,mbl->mab', head_hot, pair_weight, tail_hot, precision=...  2.49 us
    dot_general x1, matrix products, per_device(): jnp.einsum('mca,mcb->mab', as_tiles(inside_head), out_tiles, preferred_el...  2.49 us
  transfers between devices with their start and end apart: 4, of which 3 were waited for; matrix products, arithmetic and copies ran while one was open for 8% of the time, Pallas kernels for 0%

profile of v1, /device:TPU:0, one launch (start us, length us, event | category | flops | bytes accessed | tf_op | source)
XLA Modules:
  0.0 101.9 jit_solution(4818374428400599966)
XLA Ops:
  7.2 0.0 copy-start
  7.2 0.0 all-gather.3.cloned.1.call-start
  7.3 1.0 copy-done
  8.2 0.0 copy-start.5
  8.2 2.5 %convolution_select_fusion = f32[512,512]{1,0:T(8,128)} fusion(bf16[512,512]{1,0:T(8,128)(2,1)} %param.12, bf16[512,512]{1,0:T(8,128)(2,1)S(1)} %copy-done, pred[]{:T(512)S(6)} %lt.15), kind=kOutput, calls=%fused_computation | convolution fusion | flops 268697600 | bytes 2097153 | tf_op jit(solution)/shard_map/mca,mcb->mab/dot_general | solution.py:95
  10.7 0.0 all-gather.3.cloned.1.call-update
  10.7 0.0 copy-start.7
  10.7 0.0 copy-start.8
  10.8 0.0 copy-start.3
  10.8 0.0 copy-start.4
  10.8 1.5 %convolution_bitcast_fusion.1 = f32[1,512,512]{2,1,0:T(8,128)S(1)} fusion(bf16[512,512]{1,0:T(8,128)(2,1)S(1)} %copy-done, bf16[512,512]{1,0:T(8,128)(2,1)} %param.13), kind=kOutput, calls=%fused_computation.2 | convolution fusion | flops 268435456 | bytes 2097152 | tf_op jit(solution)/shard_map/mac,mbc->mab/dot_general | solution.py:87
  12.3 6.1 %collective-permute-start = (f32[1,512,512]{2,1,0:T(8,128)S(1)}, f32[1,512,512]{2,1,0:T(8,128)S(1)}, u32[]{:S(2)}, u32[]{:S(2)}) collective-permute-start(f32[1,512,512]{2,1,0:T(8,128)S(1)} %convolution_bitcast_fusion.1), channel_id=1, source_target_pairs={{0,7},{1,0},{2,1},{3,2},{4,3},{5,4},{6,5},{7,6},{8,15},{9,8},{10,9... | collective-permute-start | bytes 3145736 | tf_op jit(solution)/shard_map/ppermute | solution.py:11
  18.4 22.4 %collective-permute-done = f32[1,512,512]{2,1,0:T(8,128)S(1)} collective-permute-done((f32[1,512,512]{2,1,0:T(8,128)S(1)}, f32[1,512,512]{2,1,0:T(8,128)S(1)}, u32[]{:S(2)}, u32[]{:S(2)}) %collective-permute-start) | collective-permute-done | bytes 1048608 | tf_op jit(solution)/shard_map/ppermute | solution.py:11
  40.8 5.2 %collective-permute-start.1 = (f32[1,512,512]{2,1,0:T(8,128)S(1)}, f32[1,512,512]{2,1,0:T(8,128)S(1)}, u32[]{:S(2)}, u32[]{:S(2)}) collective-permute-start(f32[1,512,512]{2,1,0:T(8,128)S(1)} %collective-permute-done), channel_id=1, source_target_pairs={{0,7},{1,0},{2,1},{3,2},{4,3},{5,4},{6,5},{7,6},{8,15},{9,8},{10,9... | collective-permute-start | bytes 3145736 | tf_op jit(solution)/shard_map/ppermute | solution.py:11
  46.0 21.6 %collective-permute-done.1 = f32[1,512,512]{2,1,0:T(8,128)S(1)} collective-permute-done((f32[1,512,512]{2,1,0:T(8,128)S(1)}, f32[1,512,512]{2,1,0:T(8,128)S(1)}, u32[]{:S(2)}, u32[]{:S(2)}) %collective-permute-start.1) | collective-permute-done | bytes 1048608 | tf_op jit(solution)/shard_map/ppermute | solution.py:11
  67.5 0.2 add.28
  67.7 1.4 %collective-permute-start.2 = (f32[1,512,512]{2,1,0:T(8,128)S(1)}, f32[1,512,512]{2,1,0:T(8,128)}, u32[]{:S(2)}, u32[]{:S(2)}) collective-permute-start(f32[1,512,512]{2,1,0:T(8,128)S(1)} %add.28), channel_id=1, source_target_pairs={{0,6},{1,7},{2,0},{3,1},{4,2},{5,3},{6,4},{7,5},{8,14},{9,15},{10,... | collective-permute-start | bytes 3145736 | tf_op jit(solution)/shard_map/ppermute | solution.py:11
  69.1 0.0 copy-done.5
  69.1 0.6 broadcast_in_dim.7
  69.7 1.4 %mul.67 = f32[1,512,512]{2,1,0:T(8,128)} reshape(f32[512,4,128]{2,1,0:T(4,128)S(1)} %broadcast_in_dim.7) | data formatting | bytes 2097152 | tf_op jit(solution)/shard_map/mul | solution.py:38
  71.1 0.0 copy-start.1
  72.5 0.0 copy-done.7
  72.5 0.0 copy-done.8
  72.5 0.3 fusion.9
  72.8 0.0 copy-done.3
  72.8 0.3 fusion.8
  73.2 0.0 copy-done.4
  73.2 0.3 fusion.7
  73.5 0.0 all-gather.3.cloned.1.call-done
  73.6 3.8 %reduce.1 = f32[512,512]{1,0:T(8,128)} reduce(f32[4,512,512]{2,1,0:T(8,128)} %bitcast.48, f32[]{:T(128)} %constant.33.clone.1), dimensions={0}, to_apply=%region_0.1 | reduce | flops 786432 | bytes 5242884 | tf_op jit(solution)/shard_map/reduce_sum | solution.py:99
  77.3 0.0 copy-start.6
  77.3 13.8 %collective-permute-done.2 = f32[1,512,512]{2,1,0:T(8,128)} collective-permute-done((f32[1,512,512]{2,1,0:T(8,128)S(1)}, f32[1,512,512]{2,1,0:T(8,128)}, u32[]{:S(2)}, u32[]{:S(2)}) %collective-permute-start.2) | collective-permute-done | bytes 1048608 | tf_op jit(solution)/shard_map/ppermute | solution.py:11
  91.1 0.0 copy-done.1
  91.1 1.8 %fusion.6 = f32[1,512,512]{2,1,0:T(8,128)S(1)} fusion(f32[1,512,512]{2,1,0:T(8,128)S(1)} %copy-done.1, f32[512,512]{1,0:T(8,128)} %reduce.1, f32[1,512,512]{2,1,0:T(8,128)S(1)} %add.28, f32[1,512,512]{2,1,0:T(8,128)} %collective-permute-done.2, f32[512]{0:T(512)S(1)} %bitcast.54, f32[512]{0:T(512)S(1)} %bitcast.53), kind=kLoop, calls=%fused_computation.11 | loop fusion | flops 1572864 | bytes 5246976 | tf_op jit(solution)/shard_map/div | solution.py:38
  92.9 0.0 copy-start.2
  92.9 0.0 copy-done.6
  92.9 2.2 %fusion.3 = f32[512,512]{1,0:T(8,128)} fusion(f32[512,4]{1,0:T(8,128)S(1)} %fusion.7, f32[1,512,512]{2,1,0:T(8,128)S(1)} %fusion.6, f32[512,512]{1,0:T(8,128)S(1)} %copy-done.6, f32[]{:T(128)} %bitcast.47, f32[512]{0:T(512)S(1)} %iota_add_fusion, s32[512]{0:T(512)S(1)} %bitcast.56), kind=kOutput, calls=%fused_computation.6 | convolution fusion | flops 14157824 | bytes 3158020 | tf_op jit(solution)/shard_map/mak,kl,mbl->mab/dot_general | solution.py:43
  95.1 0.0 copy-done.2
  (3 shorter events, 0.0 us)
Async XLA Ops:
  7.2 1.0 %copy-start = (bf16[512,512]{1,0:T(8,128)(2,1)S(1)}, bf16[512,512]{1,0:T(8,128)(2,1)}, u32[]{:S(2)}) copy-start(bf16[512,512]{1,0:T(8,128)(2,1)} %param.11) | copy-start | bytes 1572868
  7.2 66.4 %all-gather.3.cloned.1.call-start = ((), (), s32[]{:S(2)}) async-start(), calls=%async_computation | async-start | bytes 5242880 | tf_op jit(solution)/shard_map/all_gather | solution.py:99
  8.2 60.9 %copy-start.5 = (s32[4,4]{1,0:T(4,128)S(1)}, s32[4,4]{1,0:T(4,128)}, u32[]{:S(2)}) copy-start(s32[4,4]{1,0:T(4,128)} %param.17) | copy-start | bytes 196
  10.7 61.8 %copy-start.7 = (s32[1,512]{1,0:T(1,128)S(1)}, s32[1,512]{1,0:T(1,128)}, u32[]{:S(2)}) copy-start(s32[1,512]{1,0:T(1,128)} %param.16) | copy-start | bytes 6148
  10.7 61.8 %copy-start.8 = (f32[4]{0:T(128)S(1)}, f32[4]{0:T(128)}, u32[]{:S(2)}) copy-start(f32[4]{0:T(128)} %param.18) | copy-start | bytes 52
  10.8 62.1 %copy-start.3 = (s32[1,512]{1,0:T(1,128)S(1)}, s32[1,512]{1,0:T(1,128)}, u32[]{:S(2)}) copy-start(s32[1,512]{1,0:T(1,128)} %param.15) | copy-start | bytes 6148
  10.8 62.4 %copy-start.4 = (f32[4,4]{1,0:T(4,128)S(1)}, f32[4,4]{1,0:T(4,128)}, u32[]{:S(2)}) copy-start(f32[4,4]{1,0:T(4,128)} %param.19) | copy-start | bytes 196
  12.3 28.5 %collective-permute-start = (f32[1,512,512]{2,1,0:T(8,128)S(1)}, f32[1,512,512]{2,1,0:T(8,128)S(1)}, u32[]{:S(2)}, u32[]{:S(2)}) collective-permute-start(f32[1,512,512]{2,1,0:T(8,128)S(1)} %convolution_bitcast_fusion.1), channel_id=1, source_target_pairs={{0,7},{1,0},{2,1},{3,2},{4,3},{5,4},{6,5},{7,6},{8,15},{9,8},{10,9... | collective-permute-start | bytes 3145736 | tf_op jit(solution)/shard_map/ppermute | solution.py:11
  40.8 26.7 %collective-permute-start.1 = (f32[1,512,512]{2,1,0:T(8,128)S(1)}, f32[1,512,512]{2,1,0:T(8,128)S(1)}, u32[]{:S(2)}, u32[]{:S(2)}) collective-permute-start(f32[1,512,512]{2,1,0:T(8,128)S(1)} %collective-permute-done), channel_id=1, source_target_pairs={{0,7},{1,0},{2,1},{3,2},{4,3},{5,4},{6,5},{7,6},{8,15},{9,8},{10,9... | collective-permute-start | bytes 3145736 | tf_op jit(solution)/shard_map/ppermute | solution.py:11
  67.7 23.3 %collective-permute-start.2 = (f32[1,512,512]{2,1,0:T(8,128)S(1)}, f32[1,512,512]{2,1,0:T(8,128)}, u32[]{:S(2)}, u32[]{:S(2)}) collective-permute-start(f32[1,512,512]{2,1,0:T(8,128)S(1)} %add.28), channel_id=1, source_target_pairs={{0,6},{1,7},{2,0},{3,1},{4,2},{5,3},{6,4},{7,5},{8,14},{9,15},{10,... | collective-permute-start | bytes 3145736 | tf_op jit(solution)/shard_map/ppermute | solution.py:11
  71.1 20.0 %copy-start.1 = (f32[1,512,512]{2,1,0:T(8,128)S(1)}, f32[1,512,512]{2,1,0:T(8,128)}, u32[]{:S(2)}) copy-start(f32[1,512,512]{2,1,0:T(8,128)} %mul.67) | copy-start | bytes 3145732
  77.3 15.6 %copy-start.6 = (f32[512,512]{1,0:T(8,128)S(1)}, f32[512,512]{1,0:T(8,128)}, u32[]{:S(2)}) copy-start(f32[512,512]{1,0:T(8,128)} %param.14) | copy-start | bytes 3145732
  92.9 2.2 %copy-start.2 = (f32[1,512,512]{2,1,0:T(8,128)}, f32[1,512,512]{2,1,0:T(8,128)S(1)}, u32[]{:S(2)}) copy-start(f32[1,512,512]{2,1,0:T(8,128)S(1)} %fusion.6) | copy-start | bytes 3145732
Sparse Core Ops, SparseCore 0:
  10.8 37.1 all-gather.2
